TPU v7x, 32 devices: a whole 2x2x4 slice. The times are simulated.
32 devices in a mesh: dp: 4 (over x, core), fsdp: 8 (over z, y).
Axes of the slice: x: 2, y: 2, z: 4, core: 2. Of those that a mesh axis runs over, the one named last changes fastest.
Arguments:
- queries: bfloat16 [64, 128, 1280], P(('dp', 'fsdp')), may hold values from -100 to 100
- keys: bfloat16 [64, 128, 1280], P(('dp', 'fsdp')), may hold values from -100 to 100
- values: bfloat16 [64, 128, 1280], P(('dp', 'fsdp')), may hold values from -64 to 64
- block_len: int32 [64], P(('dp', 'fsdp')), may hold values from 0 to 128, as said below
- target: int32 [64], P(('dp', 'fsdp')), may hold values from 0 to 2, as said below
- cotangent: bfloat16 [32, 128, 1280], P(('dp', 'fsdp')), may hold values from -6 to 6
- out_weight: bfloat16 [1280, 1280], P('fsdp'), may hold values from -0.15625 to 0.15625
Outputs:
- embedding: bfloat16 [32, 128, 1280], P(('dp', 'fsdp'))
- weight_grad: float32 [1280, 1280], P('fsdp')
Inputs may be any that keep to these rules, and one draw needn't show every extreme that they name: `block_len`: 0 exactly in the empty slots, those with target 2; live blocks hold 1 to 128 patches; in every draw some device has all its slots live and full. `target`: t < 1: output slot t of the same device; 1 <= t < 2: output slot t - 1 of the next device along dp (wrapping), same fsdp index; t = 2: empty slot; live values are distinct within a device, every output slot receives exactly one block, and in every draw some device has all 2 slots live.
All inputs are finite; a program needn't handle non-finite values.
Results may differ from a plain program's by a relative error of at most 0.012.
Values may be sent and summed in bfloat16 or wider, within the bound.
A program may use at most 64 MiB of HBM per device.

v0:
```python
import jax
import jax.numpy as jnp
from jax import lax
from jax.sharding import PartitionSpec as P

HEADS = 16


def from_behind(shard, axis, by):
    size = lax.axis_size(axis)
    return lax.ppermute(shard, axis, [(i, (i + by) % size) for i in range(size)])


def attend(query, key_block, value_block, length):
    blocks, window, features = query.shape
    head_dim = features // HEADS
    shape = (blocks, window, HEADS, head_dim)
    query_heads = query.reshape(shape)
    key_heads = key_block.reshape(shape)
    value_heads = value_block.reshape(shape)
    scores = jnp.einsum(
        "bqhd,bkhd->bhqk", query_heads, key_heads, preferred_element_type=jnp.float32
    ) * head_dim ** (-0.5)
    position = jnp.arange(window, dtype=jnp.int32)
    usable = position[None, :] < length[:, None]
    scores = jnp.where(usable[:, None, None, :], scores, -1e30)
    highest = jnp.max(scores, axis=-1, keepdims=True)
    exponent = jnp.exp(scores - highest)
    attn_weights = (exponent / jnp.sum(exponent, axis=-1, keepdims=True)).astype(jnp.bfloat16)
    mixed_out = jnp.einsum(
        "bhqk,bkhd->bqhd", attn_weights, value_heads, preferred_element_type=jnp.float32
    )
    mixed_out = jnp.where(usable[:, :, None, None], mixed_out, 0.0)
    return mixed_out.reshape(blocks, window, features).astype(jnp.bfloat16)


def pack_slots(target, arrays):
    slot_count = target.shape[0]
    select_map = (target[None, :] == jnp.arange(slot_count, dtype=jnp.int32)[:, None]).astype(
        jnp.bfloat16
    )
    return tuple(
        (
            jnp.einsum(
                "ts,swd->twd", select_map, array_item, preferred_element_type=jnp.float32
            ).astype(jnp.bfloat16)
            for array_item in arrays
        )
    )


def local(queries, keys, values, block_len, target, cotangent, out_weight):
    own_slots = cotangent.shape[0]
    local_out = attend(queries, keys, values, block_len)
    out_pack = pack_slots(target, (local_out,))[0]
    arrived = from_behind(out_pack[own_slots:], "dp", 1)
    attended = out_pack[:own_slots] + arrived
    features = attended.shape[-1]
    flat_rows = attended.reshape(-1, features)
    row_total = flat_rows.shape[0]
    columns = flat_rows
    projected = jnp.dot(
        columns,
        lax.all_gather(out_weight, "fsdp", axis=0, tiled=True),
        preferred_element_type=jnp.float32,
    )
    embedding = projected.astype(jnp.bfloat16).reshape(attended.shape)
    cot_rows = cotangent.reshape(row_total, features)
    columns = flat_rows
    fsdp_summed = lax.psum_scatter(
        lax.dot_general(
            columns, cot_rows, (((0,), (0,)), ((), ())), preferred_element_type=jnp.float32
        ).astype(jnp.bfloat16),
        "fsdp",
        scatter_dimension=0,
        tiled=True,
    ).astype(jnp.float32)
    summed = lax.psum(fsdp_summed, "dp")
    squares = lax.psum(jnp.sum(summed * summed), "fsdp")
    norm_value = jnp.sqrt(squares + 1e-06)
    factor = jnp.minimum(1.0, float(features) / norm_value)
    return (embedding, summed * factor)


def solution(mesh):
    placed = (
        P(("dp", "fsdp"), None, None),
        P(("dp", "fsdp"), None, None),
        P(("dp", "fsdp"), None, None),
        P(("dp", "fsdp")),
        P(("dp", "fsdp")),
        P(("dp", "fsdp"), None, None),
        P("fsdp", None),
    )
    return jax.shard_map(
        local,
        mesh=mesh,
        in_specs=placed,
        out_specs=(P(("dp", "fsdp"), None, None), P("fsdp", None)),
        check_vma=False,
    )
```

profile of v0, /device:TPU:0, one launch (start us, length us, event | category | flops | bytes accessed | tf_op | source)
XLA Modules:
  0.0 201.7 jit_solution(7435030648020174563)
XLA Ops:
  7.2 0.0 copy-start
  7.2 0.0 copy-start.1
  7.2 0.0 reduce-scatter.2.cloned.1.call-start
  7.2 0.8 iota_compare_fusion
  8.0 1.4 copy.19
  9.5 1.4 copy.20
  10.9 0.0 copy-done.1
  10.9 0.3 copy.21
  11.3 2.3 %fusion.18 = (f32[2,16,128]{2,1,0:T(8,128)S(1)}, f32[2,16,128,128]{2,3,1,0:T(8,128)}) fusion(pred[2,128]{1,0:T(4,128)(4,1)S(1)} %iota_compare_fusion, bf16[2,128,16,80]{1,3,2,0:T(8,128)(2,1)S(1)} %bitcast.25, bf16[2,128,16,80]{1,3,2,0:T(8,128)(2,1)S(1)} %bitcast.26), kind=kOutput, calls=%fused_computation.29 | convolution fusion | flops 85983360 | bytes 3424512 | tf_op jit(solution)/shard_map/sub | solution.py:28
  13.6 0.0 copy-start.2
  13.6 2.1 %fusion.3 = bf16[2,16,128,80]{2,3,1,0:T(8,128)(2,1)S(1)} fusion(bf16[2,128,16,80]{1,3,2,0:T(8,128)(2,1)S(1)} %bitcast.24, f32[2,16,128,128]{2,3,1,0:T(8,128)} %get-tuple-element.3, f32[2,16,128]{2,1,0:T(8,128)S(1)} %get-tuple-element.2, pred[2,128]{1,0:T(4,128)(4,1)S(1)} %iota_compare_fusion), kind=kOutput, calls=%fused_computation.10 | convolution fusion | flops 85590016 | bytes 3424512 | tf_op jit(solution)/shard_map/bhqk,bkhd->bqhd/dot_general | solution.py:30
  15.8 1.0 copy.23
  16.7 0.0 copy-done.2
  16.7 0.8 convolution_convert_fusion.1
  17.6 0.7 slice.9
  18.3 0.5 collective-permute-start
  18.9 6.7 %collective-permute-done = bf16[1,128,1280]{2,1,0:T(8,128)(2,1)S(1)} collective-permute-done((bf16[1,128,1280]{2,1,0:T(8,128)(2,1)S(1)}, bf16[1,128,1280]{2,1,0:T(8,128)(2,1)S(1)}, u32[]{:S(2)}, u32[]{:S(2)}) %collective-permute-start) | collective-permute-done | bytes 327712 | tf_op jit(solution)/shard_map/ppermute | solution.py:11
  25.6 0.8 slice_add_fusion
  26.3 0.0 copy-done
  26.3 2.8 %convolution_convert_fusion = bf16[1280,1280]{1,0:T(8,128)(2,1)} fusion(bf16[1,128,1280]{2,1,0:T(8,128)(2,1)S(1)} %copy-done, bf16[1,128,1280]{2,0,1:T(2,128)(2,1)S(1)} %slice_add_fusion), kind=kOutput, calls=%fused_computation.1 | convolution fusion | flops 421068800 | bytes 3932160 | tf_op jit(solution)/shard_map/dot_general | solution.py:71
  29.1 0.0 reduce-scatter.2.cloned.1.call-update
  29.1 0.0 all-gather.2.cloned.1.call-start
  29.2 0.7 all-gather.2.cloned.1.call-update
  29.9 77.8 %reduce-scatter.2.cloned.1.call-done = bf16[160,1280]{1,0:T(8,128)(2,1)} async-done(((bf16[1280,1280]{1,0:T(8,128)(2,1)}), bf16[160,1280]{1,0:T(8,128)(2,1)}) %reduce-scatter.2.cloned.1.call-update) | async-done | bytes 409616 | tf_op jit(solution)/shard_map/reduce_scatter | solution.py:70
  107.7 20.2 %all-reduce.1 = f32[160,1280]{1,0:T(8,128)S(1)} all-reduce(bf16[160,1280]{1,0:T(8,128)(2,1)} %reduce-scatter.2.cloned.1.call-done), channel_id=1, replica_groups=mesh['dp'=4,'fsdp'=8] {'dp'}, use_global_device_ids=true, to_apply=%region_3.4 | all-reduce | flops 204800 | bytes 1228800 | tf_op jit(solution)/shard_map/psum | solution.py:78
  127.9 0.8 multiply_reduce_fusion
  128.7 41.6 %all-gather.2.cloned.1.call-done = bf16[1280,1280]{1,0:T(8,128)(2,1)} async-done(((bf16[160,1280]{1,0:T(8,128)(2,1)}), bf16[1280,1280]{1,0:T(8,128)(2,1)}) %all-gather.2.cloned.1.call-update) | async-done | bytes 3276816 | tf_op jit(solution)/shard_map/all_gather | solution.py:64
  170.3 3.3 %fusion.1 = bf16[1,128,1280]{2,1,0:T(8,128)(2,1)} fusion(bf16[1280,1280]{1,0:T(8,128)(2,1)} %all-gather.2.cloned.1.call-done, bf16[1,128,1280]{2,0,1:T(2,128)(2,1)S(1)} %slice_add_fusion), kind=kOutput, calls=%fused_computation.4 | convolution fusion | flops 419594240 | bytes 3932160 | tf_op jit(solution)/shard_map/dot_general | solution.py:62
  173.5 19.7 %psum.15 = f32[]{:T(128)} all-reduce(f32[]{:T(128)} %multiply_reduce_fusion), channel_id=1, replica_groups=mesh['dp'=4,'fsdp'=8] {'fsdp'}, use_global_device_ids=true, to_apply=%region_5.6 | all-reduce | flops 1 | bytes 8 | tf_op jit(solution)/shard_map/psum | solution.py:79
  194.0 0.9 broadcast_multiply_fusion
  (1 shorter events, 0.0 us)
Async XLA Ops:
  7.2 19.2 %copy-start = (bf16[1,128,1280]{2,1,0:T(8,128)(2,1)S(1)}, bf16[1,128,1280]{2,1,0:T(8,128)(2,1)}, u32[]{:S(2)}) copy-start(bf16[1,128,1280]{2,1,0:T(8,128)(2,1)} %param.12) | copy-start | bytes 983044
  7.2 3.7 %copy-start.1 = (bf16[2,128,1280]{2,1,0:T(8,128)(2,1)S(1)}, bf16[2,128,1280]{2,1,0:T(8,128)(2,1)}, u32[]{:S(2)}) copy-start(bf16[2,128,1280]{2,1,0:T(8,128)(2,1)} %param.9) | copy-start | bytes 1966084
  7.2 100.5 %reduce-scatter.2.cloned.1.call-start = ((), (), s32[]{:S(2)}) async-start(), calls=%async_computation.2 | async-start | bytes 3686400 | tf_op jit(solution)/shard_map/reduce_scatter | solution.py:70
  13.6 3.1 %copy-start.2 = (s32[2]{0:T(128)S(1)}, s32[2]{0:T(128)}, u32[]{:S(2)}) copy-start(s32[2]{0:T(128)} %param.11) | copy-start | bytes 28
  18.3 7.2 %collective-permute-start = (bf16[1,128,1280]{2,1,0:T(8,128)(2,1)S(1)}, bf16[1,128,1280]{2,1,0:T(8,128)(2,1)S(1)}, u32[]{:S(2)}, u32[]{:S(2)}) collective-permute-start(bf16[1,128,1280]{2,1,0:T(8,128)(2,1)S(1)} %copy.24), channel_id=1, source_target_pairs={{0,8},{8,16},{16,24},{24,0},{1,9},{9,17},{17,25},{25,1},{2,10},{10... | collective-permute-start | bytes 983048 | tf_op jit(solution)/shard_map/ppermute | solution.py:11
  29.1 141.2 %all-gather.2.cloned.1.call-start = ((), (), s32[]{:S(2)}) async-start(), calls=%async_computation.1 | async-start | bytes 3686400 | tf_op jit(solution)/shard_map/all_gather | solution.py:64
Sparse Core Ops, SparseCore 0:
  29.2 78.3 reduce-scatter.1
  109.8 60.3 all-gather.1
where the time goes:
time: 202 us
  waiting for transfers between devices  127 us (63%)
  blocking collectives  40 us (20%)
  between operations  14.8 us (7%)
  matrix products  11.3 us (6%)
  local copies, waits for them, and re-layouts  4.93 us (2%)
  other arithmetic  3.32 us (2%)
    reduce_scatter x1, waiting for transfers between devices, local(): lax.psum_scatter(lax.dot_general(columns, cot_rows, (((0,), (0,)), ((), (...  77.8 us
    all_gather x1, waiting for transfers between devices, local(): lax.all_gather(out_weight, 'fsdp', axis=0, tiled=True)  41.6 us
    psum x1, blocking collectives, local(): summed = lax.psum(fsdp_summed, 'dp')  20.2 us
    psum x1, blocking collectives, local(): squares = lax.psum(jnp.sum(summed * summed), 'fsdp')  19.7 us
    ppermute x1, waiting for transfers between devices, from_behind(): lax.ppermute(shard, axis, [(i, (i + by) % size) for i in range(size)])  6.68 us
  transfers between devices with their start and end apart: 3, of which 3 were waited for; matrix products, arithmetic and copies ran while one was open for 0% of the time, Pallas kernels for 0%

commit v1 on v0

--- a/solution.py
+++ b/solution.py
@@ -4,6 +4,18 @@
 from jax.sharding import PartitionSpec as P
 
 HEADS = 16
+
+
+def collect(x, axis, dim):
+    ways, here, step = (lax.axis_size(axis), lax.axis_index(axis), x.shape[dim])
+    line, have = (x, 1)
+    while have < ways:
+        line = jnp.concatenate(
+            [line, lax.ppermute(line, axis, [(d, (d - have) % ways) for d in range(ways)])],
+            axis=dim,
+        )
+        have = 2 * have
+    return jnp.roll(line, here * step, axis=dim)
 
 
 def from_behind(shard, axis, by):
@@ -59,11 +71,7 @@
     flat_rows = attended.reshape(-1, features)
     row_total = flat_rows.shape[0]
     columns = flat_rows
-    projected = jnp.dot(
-        columns,
-        lax.all_gather(out_weight, "fsdp", axis=0, tiled=True),
-        preferred_element_type=jnp.float32,
-    )
+    projected = jnp.dot(columns, collect(out_weight, "fsdp", 0), preferred_element_type=jnp.float32)
     embedding = projected.astype(jnp.bfloat16).reshape(attended.shape)
     cot_rows = cotangent.reshape(row_total, features)
     columns = flat_rows

time: 202 us -> 234 us (1.16)
  local copies, waits for them, and re-layouts: 4.93 us -> 16.5 us
  waiting for transfers between devices: 127 us -> 138 us
  starting transfers between devices: 0.62 us -> 6.06 us
    ppermute x0 -> x3, waiting for transfers between devices: none -> 131 us  [collect(): lax.ppermute(line, axis, [(d, (d - have) % ways) for d in range(ways)])]
    reduce_scatter x1, waiting for transfers between devices: 77.8 us -> 0.01 us  [local(): lax.psum_scatter(lax.dot_general(columns, cot_rows, (((0,), (0,)), ((), (...]
    all_gather x1 -> x0, waiting for transfers between devices: 41.6 us -> none  [local(): lax.all_gather(out_weight, 'fsdp', axis=0, tiled=True)]
    unnamed x9 -> x16, local copies, waits for them, and re-layouts: 3.22 us -> 12 us
    ppermute x0 -> x3, starting transfers between devices: none -> 5.48 us  [collect(): lax.ppermute(line, axis, [(d, (d - have) % ways) for d in range(ways)])]
    concatenate x0 -> x1, local copies, waits for them, and re-layouts: none -> 2.74 us  [collect(): return jnp.roll(line, here * step, axis=dim)]
    psum x1, blocking collectives: 19.7 us -> 22.2 us  [local(): squares = lax.psum(jnp.sum(summed * summed), 'fsdp')]
  transfers between devices with their start and end apart: 3 -> 5, of which waited for: 3 -> 4; matrix products, arithmetic and copies ran while one was open for 0% -> 5% of each run, Pallas kernels for 0% -> 0%
where the time goes in v1:
time: 234 us
  waiting for transfers between devices  138 us (59%)
  blocking collectives  41.7 us (18%)
  local copies, waits for them, and re-layouts  16.5 us (7%)
  between operations  14.9 us (6%)
  matrix products  11.8 us (5%)
  starting transfers between devices  6.06 us (3%)
  other arithmetic  4.61 us (2%)
    ppermute x3, waiting for transfers between devices, collect(): lax.ppermute(line, axis, [(d, (d - have) % ways) for d in range(ways)])  131 us
    psum x1, blocking collectives, local(): squares = lax.psum(jnp.sum(summed * summed), 'fsdp')  22.2 us
    psum x1, blocking collectives, local(): summed = lax.psum(fsdp_summed, 'dp')  19.5 us
    unnamed x16, local copies, waits for them, and re-layouts  12 us
    ppermute x1, waiting for transfers between devices, from_behind(): lax.ppermute(shard, axis, [(i, (i + by) % size) for i in range(size)])  6.67 us
    ppermute x3, starting transfers between devices, collect(): lax.ppermute(line, axis, [(d, (d - have) % ways) for d in range(ways)])  5.48 us
  transfers between devices with their start and end apart: 5, of which 4 were waited for; matrix products, arithmetic and copies ran while one was open for 5% of the time, Pallas kernels for 0%

profile of v1, /device:TPU:0, one launch (start us, length us, event | category | flops | bytes accessed | tf_op | source)
XLA Modules:
  0.0 233.6 jit_solution(8576842461800839065)
XLA Ops:
  7.2 1.4 copy.21
  8.7 0.7 iota_compare_fusion
  9.4 1.4 copy.19
  10.8 1.4 copy.20
  12.3 2.3 %fusion.26 = (f32[2,16,128]{2,1,0:T(8,128)S(1)}, f32[2,16,128,128]{2,3,1,0:T(8,128)}) fusion(pred[2,128]{1,0:T(4,128)(4,1)S(1)} %iota_compare_fusion, bf16[2,128,16,80]{1,3,2,0:T(8,128)(2,1)S(1)} %bitcast.25, bf16[2,128,16,80]{1,3,2,0:T(8,128)(2,1)S(1)} %bitcast.26), kind=kOutput, calls=%fused_computation.42 | convolution fusion | flops 85983360 | bytes 3424512 | tf_op jit(solution)/shard_map/sub | solution.py:40
  14.6 2.1 fusion.10
  16.7 1.0 copy.23
  17.7 0.8 convolution_convert_fusion.1
  18.6 0.7 slice.9
  19.3 0.5 collective-permute-start
  19.9 6.7 %collective-permute-done = bf16[1,128,1280]{2,1,0:T(8,128)(2,1)S(1)} collective-permute-done((bf16[1,128,1280]{2,1,0:T(8,128)(2,1)S(1)}, bf16[1,128,1280]{2,1,0:T(8,128)(2,1)S(1)}, u32[]{:S(2)}, u32[]{:S(2)}) %collective-permute-start) | collective-permute-done | bytes 327712 | tf_op jit(solution)/shard_map/ppermute | solution.py:23
  26.5 0.8 slice_add_fusion
  27.3 2.8 %convolution_convert_fusion = bf16[1280,1280]{1,0:T(8,128)(2,1)} fusion(bf16[1,128,1280]{2,1,0:T(8,128)(2,1)S(1)} %copy-done, bf16[1,128,1280]{2,0,1:T(2,128)(2,1)S(1)} %slice_add_fusion), kind=kOutput, calls=%fused_computation.1 | convolution fusion | flops 421068800 | bytes 3932160 | tf_op jit(solution)/shard_map/dot_general | solution.py:79
  30.2 5.4 %collective-permute-start.1 = (bf16[160,1280]{1,0:T(8,128)(2,1)S(1)}, bf16[160,1280]{1,0:T(8,128)(2,1)S(1)}, u32[]{:S(2)}, u32[]{:S(2)}) collective-permute-start(bf16[160,1280]{1,0:T(8,128)(2,1)S(1)} %copy-done.1), channel_id=1, source_target_pairs={{0,7},{1,0},{2,1},{3,2},{4,3},{5,4},{6,5},{7,6},{8,15},{9,8},{10,9... | collective-permute-start | bytes 1228808 | tf_op jit(solution)/shard_map/ppermute | solution.py:14
  35.6 15.7 %collective-permute-done.1 = bf16[160,1280]{1,0:T(8,128)(2,1)S(1)} collective-permute-done((bf16[160,1280]{1,0:T(8,128)(2,1)S(1)}, bf16[160,1280]{1,0:T(8,128)(2,1)S(1)}, u32[]{:S(2)}, u32[]{:S(2)}) %collective-permute-start.1) | collective-permute-done | bytes 409632 | tf_op jit(solution)/shard_map/ppermute | solution.py:14
  51.4 0.1 collective-permute-start.2
  51.4 35.4 %collective-permute-done.2 = bf16[320,1280]{1,0:T(8,128)(2,1)S(1)} collective-permute-done((bf16[320,1280]{1,0:T(8,128)(2,1)S(1)}, bf16[320,1280]{1,0:T(8,128)(2,1)S(1)}, u32[]{:S(2)}, u32[]{:S(2)}) %collective-permute-start.2) | collective-permute-done | bytes 819232 | tf_op jit(solution)/shard_map/ppermute | solution.py:14
  86.9 1.3 pad_maximum_fusion
  88.2 0.8 constant_dynamic-update-slice_fusion.7
  89.0 0.8 constant_dynamic-update-slice_fusion.6
  89.7 1.0 constant_dynamic-update-slice_fusion.5
  90.7 80.2 %collective-permute-done.3 = bf16[640,1280]{1,0:T(8,128)(2,1)} collective-permute-done((bf16[640,1280]{1,0:T(8,128)(2,1)}, bf16[640,1280]{1,0:T(8,128)(2,1)}, u32[]{:S(2)}, u32[]{:S(2)}) %collective-permute-start.3) | collective-permute-done | bytes 1638432 | tf_op jit(solution)/shard_map/ppermute | solution.py:14
  170.9 2.7 %constant_dynamic-update-slice_fusion.4 = bf16[2560,1280]{1,0:T(8,128)(2,1)} fusion(bf16[2560,1280]{1,0:T(8,128)(2,1)} %constant_dynamic-update-slice_fusion.5, bf16[640,1280]{1,0:T(8,128)(2,1)} %collective-permute-done.3), kind=kLoop, calls=%fused_computation.31 | loop fusion | bytes 3276800
  173.6 0.8 constant_dynamic-update-slice_fusion.3
  174.4 0.8 constant_dynamic-update-slice_fusion.2
  175.2 0.9 constant_dynamic-update-slice_fusion.1
  176.1 2.7 %constant_dynamic-update-slice_fusion = bf16[2560,1280]{1,0:T(8,128)(2,1)} fusion(bf16[2560,1280]{1,0:T(8,128)(2,1)} %constant_dynamic-update-slice_fusion.1, bf16[640,1280]{1,0:T(8,128)(2,1)} %collective-permute-done.3), kind=kLoop, calls=%fused_computation.27 | loop fusion | bytes 3276800 | tf_op jit(solution)/shard_map/jit(_roll_dynamic)/concatenate | solution.py:18
  178.9 19.5 %all-reduce.1 = f32[160,1280]{1,0:T(8,128)S(1)} all-reduce(bf16[160,1280]{1,0:T(8,128)(2,1)} %reduce-scatter.2.cloned.1.call-done), channel_id=1, replica_groups=mesh['dp'=4,'fsdp'=8] {'dp'}, use_global_device_ids=true, to_apply=%region_3.4 | all-reduce | flops 204800 | bytes 1228800 | tf_op jit(solution)/shard_map/psum | solution.py:86
  198.4 0.8 multiply_reduce_fusion
  199.2 3.7 %fusion.6 = bf16[1,128,1280]{2,1,0:T(8,128)(2,1)} fusion(bf16[2560,1280]{1,0:T(8,128)(2,1)} %constant_dynamic-update-slice_fusion, s32[]{:T(128)S(6)} %select_n.25, bf16[1,128,1280]{2,0,1:T(2,128)(2,1)S(1)} %slice_add_fusion), kind=kOutput, calls=%fused_computation.6 | convolution fusion | flops 419594240 | bytes 3932164 | tf_op jit(solution)/shard_map/dot_general | solution.py:74
  202.9 22.2 %psum.15 = f32[]{:T(128)} all-reduce(f32[]{:T(128)} %multiply_reduce_fusion), channel_id=1, replica_groups=mesh['dp'=4,'fsdp'=8] {'fsdp'}, use_global_device_ids=true, to_apply=%region_5.6 | all-reduce | flops 1 | bytes 8 | tf_op jit(solution)/shard_map/psum | solution.py:87
  225.8 0.9 broadcast_multiply_fusion
  (12 shorter events, 0.2 us)
Async XLA Ops:
  7.2 20.1 %copy-start = (bf16[1,128,1280]{2,1,0:T(8,128)(2,1)S(1)}, bf16[1,128,1280]{2,1,0:T(8,128)(2,1)}, u32[]{:S(2)}) copy-start(bf16[1,128,1280]{2,1,0:T(8,128)(2,1)} %param.12) | copy-start | bytes 983044
  7.2 171.7 %reduce-scatter.2.cloned.1.call-start = ((), (), s32[]{:S(2)}) async-start(), calls=%async_computation.1 | async-start | bytes 3686400 | tf_op jit(solution)/shard_map/reduce_scatter | solution.py:78
  14.6 3.1 %copy-start.2 = (s32[2]{0:T(128)S(1)}, s32[2]{0:T(128)}, u32[]{:S(2)}) copy-start(s32[2]{0:T(128)} %param.11) | copy-start | bytes 28
  19.3 7.2 %collective-permute-start = (bf16[1,128,1280]{2,1,0:T(8,128)(2,1)S(1)}, bf16[1,128,1280]{2,1,0:T(8,128)(2,1)S(1)}, u32[]{:S(2)}, u32[]{:S(2)}) collective-permute-start(bf16[1,128,1280]{2,1,0:T(8,128)(2,1)S(1)} %copy.24), channel_id=1, source_target_pairs={{0,8},{8,16},{16,24},{24,0},{1,9},{9,17},{17,25},{25,1},{2,10},{10... | collective-permute-start | bytes 983048 | tf_op jit(solution)/shard_map/ppermute | solution.py:23
  27.3 2.8 %copy-start.1 = (bf16[160,1280]{1,0:T(8,128)(2,1)S(1)}, bf16[160,1280]{1,0:T(8,128)(2,1)}, u32[]{:S(2)}) copy-start(bf16[160,1280]{1,0:T(8,128)(2,1)} %param.13) | copy-start | bytes 1228804
  30.2 21.2 %collective-permute-start.1 = (bf16[160,1280]{1,0:T(8,128)(2,1)S(1)}, bf16[160,1280]{1,0:T(8,128)(2,1)S(1)}, u32[]{:S(2)}, u32[]{:S(2)}) collective-permute-start(bf16[160,1280]{1,0:T(8,128)(2,1)S(1)} %copy-done.1), channel_id=1, source_target_pairs={{0,7},{1,0},{2,1},{3,2},{4,3},{5,4},{6,5},{7,6},{8,15},{9,8},{10,9... | collective-permute-start | bytes 1228808 | tf_op jit(solution)/shard_map/ppermute | solution.py:14
  51.4 35.5 %collective-permute-start.2 = (bf16[320,1280]{1,0:T(8,128)(2,1)S(1)}, bf16[320,1280]{1,0:T(8,128)(2,1)S(1)}, u32[]{:S(2)}, u32[]{:S(2)}) collective-permute-start(bf16[320,1280]{1,0:T(8,128)(2,1)S(1)} %pad_maximum_fusion.1), channel_id=1, source_target_pairs={{0,6},{1,7},{2,0},{3,1},{4,2},{5,3},{6,4},{7,5},{8,14},{9,15},{10,... | collective-permute-start | bytes 2457608 | tf_op jit(solution)/shard_map/ppermute | solution.py:14
  88.2 82.7 %collective-permute-start.3 = (bf16[640,1280]{1,0:T(8,128)(2,1)}, bf16[640,1280]{1,0:T(8,128)(2,1)}, u32[]{:S(2)}, u32[]{:S(2)}) collective-permute-start(bf16[640,1280]{1,0:T(8,128)(2,1)} %pad_maximum_fusion), channel_id=1, source_target_pairs={{0,4},{1,5},{2,6},{3,7},{4,0},{5,1},{6,2},{7,3},{8,12},{9,13},{10,... | collective-permute-start | bytes 4915208 | tf_op jit(solution)/shard_map/ppermute | solution.py:14
Sparse Core Ops, SparseCore 0:
  30.3 140.8 reduce-scatter.1
